TPU v7x, 512 devices: a whole 4x4x16 slice. The times are simulated.
512 devices in a mesh: sub: 16 (over z), leaf: 32 (over y, x, core).
Axes of the slice: x: 4, y: 4, z: 16, core: 2. Of those that a mesh axis runs over, the one named last changes fastest.
Arguments:
- shift: float32 [1], replicated, may hold values from 0.5 to 2
- self_terms: float32 [524288], P(('leaf', 'sub')), may hold values from 1 to 2
- order: int32 [512, 1024], P(('leaf', 'sub')), may hold values from 0 to 1023, each once within a row
- split: int32 [512], P(('leaf', 'sub')), may hold values from 256 to 768
- coupling: bfloat16 [524288, 768], P(('leaf', 'sub')), as said below
- higher: bfloat16 [524288, 512], P(('leaf', 'sub'))
Outputs:
- applied_higher: bfloat16 [524288, 512], P(('leaf', 'sub'))
Inputs may be any that keep to these rules, and one draw needn't show every extreme that they name: `coupling`: at every node of every level, the symmetric matrix made of diag and the blocks U V^T and V U^T of this and lower levels is positive definite.
All inputs are finite; a program needn't handle non-finite values.
Results may differ from a plain program's by a relative error of at most 0.001.
The roundings to bfloat16 on the way count: a program that leaves them out, or rounds other values in their place, can miss the bound.
Values sent between devices are 32-bit elements; how exact they have to be, the bound alone decides.
A program may use at most 64 MiB of HBM per device.

v0:
```python
import jax
import jax.numpy as jnp
from jax import lax
from jax.sharding import PartitionSpec as P

RANK = 128


def from_partner(value, axis, stride):
    mask = 2**stride
    pairs = [(source, source ^ mask) for source in range(lax.axis_size(axis))]
    return lax.ppermute(value, axis, pairs)


def factor_solve(factor, target):
    lower_part = lax.linalg.triangular_solve(factor, target, left_side=True, lower=True)
    return lax.linalg.triangular_solve(
        factor, lower_part, left_side=True, lower=True, transpose_a=True
    )


def core_terms(left_sum, right_sum):
    width = left_sum.shape[0]
    first = left_sum[:, :width]
    projected = left_sum[:, width:]
    second = right_sum[:, :width]
    beyond = right_sum[:, width:]
    identity_block = jnp.eye(width, dtype=jnp.float32)
    first_factor = jnp.linalg.cholesky(first)
    first_inverse = factor_solve(first_factor, identity_block)
    schur_factor = jnp.linalg.cholesky(first_inverse - second)
    target = beyond - jnp.dot(second, projected, precision=lax.Precision.HIGHEST)
    back = factor_solve(schur_factor, target) - projected
    across = beyond + jnp.dot(second, back, precision=lax.Precision.HIGHEST)
    return (across, back)


def project_rows(basis, columns):
    return lax.dot_general(
        basis, columns, (((0,), (0,)), ((), ())), preferred_element_type=jnp.float32
    )


def node_step(columns, mine, other, is_left):
    left_sum = jnp.where(is_left, mine, other)
    right_sum = jnp.where(is_left, other, mine)
    across, back = core_terms(left_sum, right_sum)
    coefficient = jnp.where(is_left, -across, back).astype(jnp.bfloat16)
    update = columns[:, RANK:].astype(jnp.float32) + jnp.dot(
        columns[:, :RANK], coefficient, preferred_element_type=jnp.float32
    )
    return update.astype(jnp.bfloat16)


def per_device(shift, self_terms, order, split, coupling, higher):
    sub_bits = lax.axis_size("sub").bit_length() - 1
    diagonal = shift[0] + self_terms
    joined = jnp.concatenate([coupling, higher], axis=1).astype(jnp.float32)
    columns = (joined / diagonal[:, None]).astype(jnp.bfloat16)
    inside = (order[0] < split[0]).astype(jnp.bfloat16)[:, None]
    outside = 1 - inside
    basis = coupling[:, :RANK]
    left_sum = project_rows(basis * inside, columns)
    right_sum = project_rows(basis * outside, columns)
    across, back = core_terms(left_sum, right_sum)
    own = columns[:, :RANK]
    update = columns[:, RANK:].astype(jnp.float32)
    update = update + jnp.dot(
        own * inside, (-across).astype(jnp.bfloat16), preferred_element_type=jnp.float32
    )
    update = update + jnp.dot(
        own * outside, back.astype(jnp.bfloat16), preferred_element_type=jnp.float32
    )
    columns = update.astype(jnp.bfloat16)
    position = lax.axis_index("sub")
    for level in range(1, sub_bits + 1):
        basis = coupling[:, level * RANK : (level + 1) * RANK]
        partial_value = project_rows(basis, columns)
        stride = 2 ** (level - 1)
        mine = partial_value
        for bit in range(level - 1):
            mine = mine + from_partner(mine, "sub", bit)
        other = from_partner(mine, "sub", level - 1)
        is_left = position // stride % 2 == 0
        columns = node_step(columns, mine, other, is_left)
    top = sub_bits + 1
    basis = coupling[:, top * RANK : (top + 1) * RANK]
    partial_value = project_rows(basis, columns)
    mine = lax.psum(partial_value, "sub")
    other = from_partner(mine, "leaf", 0)
    is_left = lax.axis_index("leaf") % 2 == 0
    return node_step(columns, mine, other, is_left)


def solution(mesh):
    in_specs = (
        P(),
        P(("leaf", "sub")),
        P(("leaf", "sub"), None),
        P(("leaf", "sub")),
        P(("leaf", "sub"), None),
        P(("leaf", "sub"), None),
    )
    out_specs = P(("leaf", "sub"), None)
    return jax.shard_map(
        per_device, mesh=mesh, in_specs=in_specs, out_specs=out_specs, check_vma=False
    )
```

profile of v0, /device:TPU:1, one launch (start us, length us, event | category | flops | bytes accessed | tf_op | source)
XLA Modules:
  0.0 782.3 jit_solution(3534729396626597273)
XLA Ops:
  9.2 2.3 divide_convert_fusion
  11.6 1.6 fusion.35
  13.2 1.6 fusion.37
  17.2 11.7 %cholesky.194 = f32[128,128]{1,0:T(8,128)S(1)} custom-call(f32[128,128]{1,0:T(8,128)S(1)} %fusion.114), custom_call_target="Cholesky" | custom-call | tf_op jit(solution)/shard_map/jit(cholesky)/cholesky | solution.py:29
  30.1 9.8 %custom-call.55 = f32[1,128,128]{1,2,0:T(8,128)S(1)} custom-call(f32[1,128,128]{2,1,0:T(8,128)S(1)} %fusion.61), custom_call_target="InvertDiagBlocksLowerTriangular" | custom-call | tf_op jit(solution)/shard_map/triangular_solve/custom-call.2 | solution.py:17
  42.2 11.7 %cholesky.205 = f32[128,128]{1,0:T(8,128)S(1)} custom-call(f32[128,128]{1,0:T(8,128)S(1)} %fusion.111), custom_call_target="Cholesky" | custom-call | tf_op jit(solution)/shard_map/jit(cholesky)/cholesky | solution.py:31
  55.4 9.8 %custom-call.38 = f32[1,128,128]{1,2,0:T(8,128)S(1)} custom-call(f32[1,128,128]{2,1,0:T(8,128)S(1)} %fusion.62), custom_call_target="InvertDiagBlocksLowerTriangular" | custom-call | tf_op jit(solution)/shard_map/triangular_solve | solution.py:17
  65.2 1.7 fusion.109
  67.6 1.7 fusion.2
  71.0 2.0 convolution_bitcast_fusion
  73.0 4.4 collective-permute-start
  77.4 8.5 %collective-permute-done = f32[128,1152]{0,1:T(8,128)S(1)} collective-permute-done((f32[128,1152]{0,1:T(8,128)S(1)}, f32[128,1152]{0,1:T(8,128)S(1)}, u32[]{:S(2)}, u32[]{:S(2)}) %collective-permute-start) | collective-permute-done | bytes 589856 | tf_op jit(solution)/shard_map/ppermute | solution.py:12
  86.1 11.7 %cholesky.216 = f32[128,128]{1,0:T(8,128)S(1)} custom-call(f32[128,128]{1,0:T(8,128)S(1)} %fusion.107), custom_call_target="Cholesky" | custom-call | tf_op jit(solution)/shard_map/jit(cholesky)/cholesky | solution.py:29
  99.2 9.8 %custom-call.57 = f32[1,128,128]{1,2,0:T(8,128)S(1)} custom-call(f32[1,128,128]{2,1,0:T(8,128)S(1)} %fusion.63), custom_call_target="InvertDiagBlocksLowerTriangular" | custom-call | tf_op jit(solution)/shard_map/triangular_solve/custom-call.2 | solution.py:17
  110.3 11.7 %cholesky.227 = f32[128,128]{1,0:T(8,128)S(1)} custom-call(f32[128,128]{1,0:T(8,128)S(1)} %fusion.104), custom_call_target="Cholesky" | custom-call | tf_op jit(solution)/shard_map/jit(cholesky)/cholesky | solution.py:31
  123.3 21.7 %custom-call.39 = f32[1,128,128]{1,2,0:T(8,128)S(1)} custom-call(f32[1,128,128]{2,1,0:T(8,128)S(1)} %fusion.64), custom_call_target="InvertDiagBlocksLowerTriangular" | custom-call | tf_op jit(solution)/shard_map/triangular_solve | solution.py:17
  147.3 2.4 add_convert_fusion
  151.0 4.1 collective-permute-start.1
  155.1 7.0 collective-permute-done.1
  162.2 12.1 %collective-permute-start.2 = (f32[128,1024]{0,1:T(8,128)S(1)}, f32[128,1024]{0,1:T(8,128)}, u32[]{:S(2)}, u32[]{:S(2)}) collective-permute-start(f32[128,1024]{0,1:T(8,128)S(1)} %add.127), channel_id=1, source_target_pairs={{0,64},{32,96},{64,0},{96,32},{128,192},{160,224},{192,128},{224,1... | collective-permute-start | bytes 1572872 | tf_op jit(solution)/shard_map/ppermute | solution.py:12
  174.4 22.8 %collective-permute-done.2 = f32[128,1024]{0,1:T(8,128)} collective-permute-done((f32[128,1024]{0,1:T(8,128)S(1)}, f32[128,1024]{0,1:T(8,128)}, u32[]{:S(2)}, u32[]{:S(2)}) %collective-permute-start.2) | collective-permute-done | bytes 524320 | tf_op jit(solution)/shard_map/ppermute | solution.py:12
  198.5 11.7 %cholesky.238 = f32[128,128]{1,0:T(8,128)S(1)} custom-call(f32[128,128]{1,0:T(8,128)S(1)} %fusion.100), custom_call_target="Cholesky" | custom-call | tf_op jit(solution)/shard_map/jit(cholesky)/cholesky | solution.py:29
  211.6 9.8 %custom-call.59 = f32[1,128,128]{1,2,0:T(8,128)S(1)} custom-call(f32[1,128,128]{2,1,0:T(8,128)S(1)} %fusion.65), custom_call_target="InvertDiagBlocksLowerTriangular" | custom-call | tf_op jit(solution)/shard_map/triangular_solve/custom-call.2 | solution.py:17
  222.6 11.7 %cholesky.249 = f32[128,128]{1,0:T(8,128)S(1)} custom-call(f32[128,128]{1,0:T(8,128)S(1)} %fusion.97), custom_call_target="Cholesky" | custom-call | tf_op jit(solution)/shard_map/jit(cholesky)/cholesky | solution.py:31
  235.7 10.2 %custom-call.40 = f32[1,128,128]{1,2,0:T(8,128)S(1)} custom-call(f32[1,128,128]{2,1,0:T(8,128)S(1)} %fusion.66), custom_call_target="InvertDiagBlocksLowerTriangular" | custom-call | tf_op jit(solution)/shard_map/triangular_solve | solution.py:17
  247.9 2.2 add_convert_fusion.1
  250.9 2.9 collective-permute-start.3
  253.8 9.7 %collective-permute-done.3 = f32[128,896]{0,1:T(8,128)S(1)} collective-permute-done((f32[128,896]{0,1:T(8,128)S(1)}, f32[128,896]{0,1:T(8,128)S(1)}, u32[]{:S(2)}, u32[]{:S(2)}) %collective-permute-start.3) | collective-permute-done | bytes 458784 | tf_op jit(solution)/shard_map/ppermute | solution.py:12
  263.6 5.7 collective-permute-start.4
  269.3 19.9 %collective-permute-done.4 = f32[128,896]{0,1:T(8,128)S(1)} collective-permute-done((f32[128,896]{0,1:T(8,128)S(1)}, f32[128,896]{0,1:T(8,128)S(1)}, u32[]{:S(2)}, u32[]{:S(2)}) %collective-permute-start.4) | collective-permute-done | bytes 458784 | tf_op jit(solution)/shard_map/ppermute | solution.py:12
  289.3 8.8 %collective-permute-start.5 = (f32[128,896]{0,1:T(8,128)S(1)}, f32[128,896]{0,1:T(8,128)S(1)}, u32[]{:S(2)}, u32[]{:S(2)}) collective-permute-start(f32[128,896]{0,1:T(8,128)S(1)} %add.132), channel_id=1, source_target_pairs={{0,128},{32,160},{64,192},{96,224},{128,0},{160,32},{192,64},{224,... | collective-permute-start | bytes 1376264 | tf_op jit(solution)/shard_map/ppermute | solution.py:12
  298.1 39.4 %collective-permute-done.5 = f32[128,896]{0,1:T(8,128)S(1)} collective-permute-done((f32[128,896]{0,1:T(8,128)S(1)}, f32[128,896]{0,1:T(8,128)S(1)}, u32[]{:S(2)}, u32[]{:S(2)}) %collective-permute-start.5) | collective-permute-done | bytes 458784 | tf_op jit(solution)/shard_map/ppermute | solution.py:12
  337.7 11.7 %cholesky.260 = f32[128,128]{1,0:T(8,128)S(1)} custom-call(f32[128,128]{1,0:T(8,128)S(1)} %fusion.93), custom_call_target="Cholesky" | custom-call | tf_op jit(solution)/shard_map/jit(cholesky)/cholesky | solution.py:29
  350.7 9.8 %custom-call.61 = f32[1,128,128]{1,2,0:T(8,128)S(1)} custom-call(f32[1,128,128]{2,1,0:T(8,128)S(1)} %fusion.67), custom_call_target="InvertDiagBlocksLowerTriangular" | custom-call | tf_op jit(solution)/shard_map/triangular_solve/custom-call.2 | solution.py:17
  361.7 11.7 %cholesky.271 = f32[128,128]{1,0:T(8,128)S(1)} custom-call(f32[128,128]{1,0:T(8,128)S(1)} %fusion.90), custom_call_target="Cholesky" | custom-call | tf_op jit(solution)/shard_map/jit(cholesky)/cholesky | solution.py:31
  374.8 9.9 %custom-call.41 = f32[1,128,128]{1,2,0:T(8,128)S(1)} custom-call(f32[1,128,128]{2,1,0:T(8,128)S(1)} %fusion.68), custom_call_target="InvertDiagBlocksLowerTriangular" | custom-call | tf_op jit(solution)/shard_map/triangular_solve | solution.py:17
  386.6 2.1 add_convert_fusion.2
  389.2 1.9 collective-permute-start.6
  391.2 10.1 %collective-permute-done.6 = f32[128,768]{0,1:T(8,128)S(1)} collective-permute-done((f32[128,768]{0,1:T(8,128)S(1)}, f32[128,768]{0,1:T(8,128)S(1)}, u32[]{:S(2)}, u32[]{:S(2)}) %collective-permute-start.6) | collective-permute-done | bytes 393248 | tf_op jit(solution)/shard_map/ppermute | solution.py:12
  401.4 1.9 collective-permute-start.7
  403.3 20.3 %collective-permute-done.7 = f32[128,768]{0,1:T(8,128)S(1)} collective-permute-done((f32[128,768]{0,1:T(8,128)S(1)}, f32[128,768]{0,1:T(8,128)S(1)}, u32[]{:S(2)}, u32[]{:S(2)}) %collective-permute-start.7) | collective-permute-done | bytes 393248 | tf_op jit(solution)/shard_map/ppermute | solution.py:12
  423.7 4.3 collective-permute-start.8
  428.0 35.9 %collective-permute-done.8 = f32[128,768]{0,1:T(8,128)S(1)} collective-permute-done((f32[128,768]{0,1:T(8,128)S(1)}, f32[128,768]{0,1:T(8,128)S(1)}, u32[]{:S(2)}, u32[]{:S(2)}) %collective-permute-start.8) | collective-permute-done | bytes 393248 | tf_op jit(solution)/shard_map/ppermute | solution.py:12
  464.7 19.0 %collective-permute-start.9 = (f32[128,768]{0,1:T(8,128)}, f32[128,768]{0,1:T(8,128)}, u32[]{:S(2)}, u32[]{:S(2)}) collective-permute-start(f32[128,768]{0,1:T(8,128)} %add.138), channel_id=1, source_target_pairs={{0,256},{32,288},{64,320},{96,352},{128,384},{160,416},{192,448},{... | collective-permute-start | bytes 1179656 | tf_op jit(solution)/shard_map/ppermute | solution.py:12
  483.7 14.6 %collective-permute-done.9 = f32[128,768]{0,1:T(8,128)} collective-permute-done((f32[128,768]{0,1:T(8,128)}, f32[128,768]{0,1:T(8,128)}, u32[]{:S(2)}, u32[]{:S(2)}) %collective-permute-start.9) | collective-permute-done | bytes 393248 | tf_op jit(solution)/shard_map/ppermute | solution.py:12
  498.3 1.9 broadcast_select_fusion.7
  500.9 1.6 copy.24
  503.9 13.2 %cholesky.282 = f32[128,128]{1,0:T(8,128)} custom-call(f32[128,128]{1,0:T(8,128)} %fusion.86), custom_call_target="Cholesky" | custom-call | tf_op jit(solution)/shard_map/jit(cholesky)/cholesky | solution.py:29
  518.6 2.1 fusion.69
  520.7 11.3 %custom-call.63 = f32[1,128,128]{1,2,0:T(8,128)} custom-call(f32[1,128,128]{2,1,0:T(8,128)} %fusion.69), custom_call_target="InvertDiagBlocksLowerTriangular" | custom-call | tf_op jit(solution)/shard_map/triangular_solve/custom-call.2 | solution.py:17
  533.1 2.1 convolution_subtract_fusion.9
  535.2 1.8 convolution_subtract_fusion.13
  537.0 1.6 copy.26
  540.1 13.2 %cholesky.293 = f32[128,128]{1,0:T(8,128)} custom-call(f32[128,128]{1,0:T(8,128)} %fusion.83), custom_call_target="Cholesky" | custom-call | tf_op jit(solution)/shard_map/jit(cholesky)/cholesky | solution.py:31
  554.8 2.1 fusion.70
  556.9 11.4 %custom-call.42 = f32[1,128,128]{1,2,0:T(8,128)} custom-call(f32[1,128,128]{2,1,0:T(8,128)} %fusion.70), custom_call_target="InvertDiagBlocksLowerTriangular" | custom-call | tf_op jit(solution)/shard_map/triangular_solve | solution.py:17
  569.9 1.5 convolution_subtract_fusion.8
  575.8 133.2 %all-reduce.2.cloned.1.call-done = f32[128,640]{0,1:T(8,128)} async-done(((f32[128,640]{0,1:T(8,128)}), f32[128,640]{0,1:T(8,128)}) %all-reduce.2.cloned.1.call-update) | async-done | bytes 327696 | tf_op jit(solution)/shard_map/psum | solution.py:89
  708.9 12.3 %collective-permute-start.10 = (f32[128,640]{0,1:T(8,128)}, f32[128,640]{0,1:T(8,128)S(1)}, u32[]{:S(2)}, u32[]{:S(2)}) collective-permute-start(f32[128,640]{0,1:T(8,128)} %all-reduce.2.cloned.1.call-done), channel_id=1, source_target_pairs={{0,1},{1,0},{2,3},{3,2},{4,5},{5,4},{6,7},{7,6},{8,9},{9,8},{10,11... | collective-permute-start | bytes 983048 | tf_op jit(solution)/shard_map/ppermute | solution.py:12
  723.9 11.7 %cholesky.304 = f32[128,128]{1,0:T(8,128)S(1)} custom-call(f32[128,128]{1,0:T(8,128)S(1)} %fusion.79), custom_call_target="Cholesky" | custom-call | tf_op jit(solution)/shard_map/jit(cholesky)/cholesky | solution.py:29
  736.9 9.8 %custom-call.65 = f32[1,128,128]{1,2,0:T(8,128)S(1)} custom-call(f32[1,128,128]{2,1,0:T(8,128)S(1)} %fusion.71), custom_call_target="InvertDiagBlocksLowerTriangular" | custom-call | tf_op jit(solution)/shard_map/triangular_solve/custom-call.2 | solution.py:17
  747.8 11.7 %cholesky.315 = f32[128,128]{1,0:T(8,128)S(1)} custom-call(f32[128,128]{1,0:T(8,128)S(1)} %fusion.76), custom_call_target="Cholesky" | custom-call | tf_op jit(solution)/shard_map/jit(cholesky)/cholesky | solution.py:31
  760.9 10.0 %custom-call.43 = f32[1,128,128]{1,2,0:T(8,128)S(1)} custom-call(f32[1,128,128]{2,1,0:T(8,128)S(1)} %fusion.72), custom_call_target="InvertDiagBlocksLowerTriangular" | custom-call | tf_op jit(solution)/shard_map/triangular_solve | solution.py:17
  772.3 2.7 add_convert_fusion.4
  (130 shorter events, 55.2 us)
Async XLA Ops:
  6.5 702.4 %all-reduce.2.cloned.1.call-start = ((), (), s32[]{:S(2)}) async-start(), calls=%async_computation | async-start | bytes 655360 | tf_op jit(solution)/shard_map/psum | solution.py:89
  14.8 0.8 copy-start.5
  71.0 2.0 copy-start
  73.0 12.9 %collective-permute-start = (f32[128,1152]{0,1:T(8,128)S(1)}, f32[128,1152]{0,1:T(8,128)S(1)}, u32[]{:S(2)}, u32[]{:S(2)}) collective-permute-start(f32[128,1152]{0,1:T(8,128)S(1)} %convolution_bitcast_fusion), channel_id=1, source_target_pairs={{0,32},{32,0},{64,96},{96,64},{128,160},{160,128},{192,224},{224,1... | collective-permute-start | bytes 1769480 | tf_op jit(solution)/shard_map/ppermute | solution.py:12
  146.7 3.0 copy-start.1
  149.7 1.4 copy-start.2
  151.0 11.1 %collective-permute-start.1 = (f32[128,1024]{0,1:T(8,128)S(1)}, f32[128,1024]{0,1:T(8,128)S(1)}, u32[]{:S(2)}, u32[]{:S(2)}) collective-permute-start(f32[128,1024]{0,1:T(8,128)S(1)} %convolution_bitcast_fusion.1), channel_id=1, source_target_pairs={{0,32},{32,0},{64,96},{96,64},{128,160},{160,128},{192,224},{224,1... | collective-permute-start | bytes 1572872 | tf_op jit(solution)/shard_map/ppermute | solution.py:12
  162.2 35.0 %collective-permute-start.2 = (f32[128,1024]{0,1:T(8,128)S(1)}, f32[128,1024]{0,1:T(8,128)}, u32[]{:S(2)}, u32[]{:S(2)}) collective-permute-start(f32[128,1024]{0,1:T(8,128)S(1)} %add.127), channel_id=1, source_target_pairs={{0,64},{32,96},{64,0},{96,32},{128,192},{160,224},{192,128},{224,1... | collective-permute-start | bytes 1572872 | tf_op jit(solution)/shard_map/ppermute | solution.py:12
  250.2 39.1 %copy-start.3 = (bf16[1024,896]{1,0:T(8,128)(2,1)}, bf16[1024,896]{1,0:T(8,128)(2,1)S(1)}, u32[]{:S(2)}) copy-start(bf16[1024,896]{1,0:T(8,128)(2,1)S(1)} %add_convert_fusion.1) | copy-start | bytes 5505028
  250.9 12.7 %collective-permute-start.3 = (f32[128,896]{0,1:T(8,128)S(1)}, f32[128,896]{0,1:T(8,128)S(1)}, u32[]{:S(2)}, u32[]{:S(2)}) collective-permute-start(f32[128,896]{0,1:T(8,128)S(1)} %convolution_bitcast_fusion.2), channel_id=1, source_target_pairs={{0,32},{32,0},{64,96},{96,64},{128,160},{160,128},{192,224},{224,1... | collective-permute-start | bytes 1376264 | tf_op jit(solution)/shard_map/ppermute | solution.py:12
  263.6 25.6 %collective-permute-start.4 = (f32[128,896]{0,1:T(8,128)S(1)}, f32[128,896]{0,1:T(8,128)S(1)}, u32[]{:S(2)}, u32[]{:S(2)}) collective-permute-start(f32[128,896]{0,1:T(8,128)S(1)} %add.131), channel_id=1, source_target_pairs={{0,64},{32,96},{64,0},{96,32},{128,192},{160,224},{192,128},{224,1... | collective-permute-start | bytes 1376264 | tf_op jit(solution)/shard_map/ppermute | solution.py:12
  289.3 48.2 %collective-permute-start.5 = (f32[128,896]{0,1:T(8,128)S(1)}, f32[128,896]{0,1:T(8,128)S(1)}, u32[]{:S(2)}, u32[]{:S(2)}) collective-permute-start(f32[128,896]{0,1:T(8,128)S(1)} %add.132), channel_id=1, source_target_pairs={{0,128},{32,160},{64,192},{96,224},{128,0},{160,32},{192,64},{224,... | collective-permute-start | bytes 1376264 | tf_op jit(solution)/shard_map/ppermute | solution.py:12
  389.2 12.1 %collective-permute-start.6 = (f32[128,768]{0,1:T(8,128)S(1)}, f32[128,768]{0,1:T(8,128)S(1)}, u32[]{:S(2)}, u32[]{:S(2)}) collective-permute-start(f32[128,768]{0,1:T(8,128)S(1)} %convolution_bitcast_fusion.3), channel_id=1, source_target_pairs={{0,32},{32,0},{64,96},{96,64},{128,160},{160,128},{192,224},{224,1... | collective-permute-start | bytes 1179656 | tf_op jit(solution)/shard_map/ppermute | solution.py:12
  401.4 22.2 %collective-permute-start.7 = (f32[128,768]{0,1:T(8,128)S(1)}, f32[128,768]{0,1:T(8,128)S(1)}, u32[]{:S(2)}, u32[]{:S(2)}) collective-permute-start(f32[128,768]{0,1:T(8,128)S(1)} %add.136), channel_id=1, source_target_pairs={{0,64},{32,96},{64,0},{96,32},{128,192},{160,224},{192,128},{224,1... | collective-permute-start | bytes 1179656 | tf_op jit(solution)/shard_map/ppermute | solution.py:12
  423.7 40.2 %collective-permute-start.8 = (f32[128,768]{0,1:T(8,128)S(1)}, f32[128,768]{0,1:T(8,128)S(1)}, u32[]{:S(2)}, u32[]{:S(2)}) collective-permute-start(f32[128,768]{0,1:T(8,128)S(1)} %add.137), channel_id=1, source_target_pairs={{0,128},{32,160},{64,192},{96,224},{128,0},{160,32},{192,64},{224,... | collective-permute-start | bytes 1179656 | tf_op jit(solution)/shard_map/ppermute | solution.py:12
  464.7 33.7 %collective-permute-start.9 = (f32[128,768]{0,1:T(8,128)}, f32[128,768]{0,1:T(8,128)}, u32[]{:S(2)}, u32[]{:S(2)}) collective-permute-start(f32[128,768]{0,1:T(8,128)} %add.138), channel_id=1, source_target_pairs={{0,256},{32,288},{64,320},{96,352},{128,384},{160,416},{192,448},{... | collective-permute-start | bytes 1179656 | tf_op jit(solution)/shard_map/ppermute | solution.py:12
  573.4 1.1 copy-start.4
  708.9 13.8 %collective-permute-start.10 = (f32[128,640]{0,1:T(8,128)}, f32[128,640]{0,1:T(8,128)S(1)}, u32[]{:S(2)}, u32[]{:S(2)}) collective-permute-start(f32[128,640]{0,1:T(8,128)} %all-reduce.2.cloned.1.call-done), channel_id=1, source_target_pairs={{0,1},{1,0},{2,3},{3,2},{4,5},{5,4},{6,7},{7,6},{8,9},{9,8},{10,11... | collective-permute-start | bytes 983048 | tf_op jit(solution)/shard_map/ppermute | solution.py:12
Sparse Core Ops, SparseCore 0:
  575.9 133.0 all-reduce.1
where the time goes:
time: 793 us; the launch traced here: 782 us
  waiting for transfers between devices  323 us (41%)
  other arithmetic  310 us (39%)
  starting transfers between devices  77.5 us (10%)
  matrix products  48.2 us (6%)
  between operations  16.1 us (2%)
    ppermute x11, waiting for transfers between devices, from_partner(): return lax.ppermute(value, axis, pairs)  190 us
    another operation x24, other arithmetic, factor_solve(): lax.linalg.triangular_solve(factor, lower_part, left_side=True, lower=Tru...  144 us
    psum x1, waiting for transfers between devices, per_device(): mine = lax.psum(partial_value, 'sub')  133 us
    ppermute x11, starting transfers between devices, from_partner(): return lax.ppermute(value, axis, pairs)  77.5 us
    another operation x18, other arithmetic, core_terms(): schur_factor = jnp.linalg.cholesky(first_inverse - second)  76.9 us
    another operation x18, other arithmetic, core_terms(): first_factor = jnp.linalg.cholesky(first)  76.6 us
  transfers between devices with their start and end apart: 12, of which 12 were waited for; matrix products, arithmetic and copies ran while one was open for 0% of the time, Pallas kernels for 0%

commit v1 on v0

--- a/solution.py
+++ b/solution.py
@@ -2,8 +2,13 @@
 import jax.numpy as jnp
 from jax import lax
 from jax.sharding import PartitionSpec as P
+from jax.lax import all_gather
 
 RANK = 128
+
+
+def racks_bring(raw, named_axis):
+    return jnp.sum(all_gather(raw, named_axis), 0)
 
 
 def from_partner(value, axis, stride):
@@ -86,7 +91,7 @@
     top = sub_bits + 1
     basis = coupling[:, top * RANK : (top + 1) * RANK]
     partial_value = project_rows(basis, columns)
-    mine = lax.psum(partial_value, "sub")
+    mine = racks_bring(partial_value, "sub")
     other = from_partner(mine, "leaf", 0)
     is_left = lax.axis_index("leaf") % 2 == 0
     return node_step(columns, mine, other, is_left)

time: 793 us -> 764 us (0.963)
  waiting for transfers between devices: 323 us -> 288 us
    psum x1 -> x0, waiting for transfers between devices: 133 us -> none  [per_device(): mine = lax.psum(partial_value, 'sub')]
    all_gather x0 -> x1, waiting for transfers between devices: none -> 98.2 us  [racks_bring(): return jnp.sum(all_gather(raw, named_axis), 0)]
where the time goes in v1:
time: 764 us; the launch traced here: 754 us
  other arithmetic  310 us (41%)
  waiting for transfers between devices  288 us (38%)
  starting transfers between devices  80.3 us (11%)
  matrix products  48.2 us (6%)
  between operations  15.9 us (2%)
  local copies, waits for them, and re-layouts  11.6 us (2%)
    ppermute x11, waiting for transfers between devices, from_partner(): return lax.ppermute(value, axis, pairs)  190 us
    another operation x24, other arithmetic, factor_solve(): lax.linalg.triangular_solve(factor, lower_part, left_side=True, lower=Tru...  144 us
    all_gather x1, waiting for transfers between devices, racks_bring(): return jnp.sum(all_gather(raw, named_axis), 0)  98.2 us
    ppermute x11, starting transfers between devices, from_partner(): return lax.ppermute(value, axis, pairs)  80.3 us
    another operation x18, other arithmetic, core_terms(): schur_factor = jnp.linalg.cholesky(first_inverse - second)  77 us
    another operation x18, other arithmetic, core_terms(): first_factor = jnp.linalg.cholesky(first)  76.6 us
  transfers between devices with their start and end apart: 12, of which 12 were waited for; matrix products, arithmetic and copies ran while one was open for 0% of the time, Pallas kernels for 0%

profile of v1, /device:TPU:1, one launch (start us, length us, event | category | flops | bytes accessed | tf_op | source)
XLA Modules:
  0.0 753.8 jit_solution(16596203525799476336)
XLA Ops:
  9.2 2.3 divide_convert_fusion
  11.6 1.6 fusion.35
  13.2 1.6 fusion.37
  17.2 11.7 %cholesky.194 = f32[128,128]{1,0:T(8,128)S(1)} custom-call(f32[128,128]{1,0:T(8,128)S(1)} %fusion.114), custom_call_target="Cholesky" | custom-call | tf_op jit(solution)/shard_map/jit(cholesky)/cholesky | solution.py:34
  30.1 9.8 %custom-call.55 = f32[1,128,128]{1,2,0:T(8,128)S(1)} custom-call(f32[1,128,128]{2,1,0:T(8,128)S(1)} %fusion.61), custom_call_target="InvertDiagBlocksLowerTriangular" | custom-call | tf_op jit(solution)/shard_map/triangular_solve/custom-call.2 | solution.py:22
  42.2 11.7 %cholesky.205 = f32[128,128]{1,0:T(8,128)S(1)} custom-call(f32[128,128]{1,0:T(8,128)S(1)} %fusion.111), custom_call_target="Cholesky" | custom-call | tf_op jit(solution)/shard_map/jit(cholesky)/cholesky | solution.py:36
  55.5 9.8 %custom-call.38 = f32[1,128,128]{1,2,0:T(8,128)S(1)} custom-call(f32[1,128,128]{2,1,0:T(8,128)S(1)} %fusion.62), custom_call_target="InvertDiagBlocksLowerTriangular" | custom-call | tf_op jit(solution)/shard_map/triangular_solve | solution.py:22
  65.3 1.7 fusion.109
  67.7 1.7 fusion.2
  71.1 2.0 convolution_bitcast_fusion
  73.1 4.4 collective-permute-start
  77.5 8.5 %collective-permute-done = f32[128,1152]{0,1:T(8,128)S(1)} collective-permute-done((f32[128,1152]{0,1:T(8,128)S(1)}, f32[128,1152]{0,1:T(8,128)S(1)}, u32[]{:S(2)}, u32[]{:S(2)}) %collective-permute-start) | collective-permute-done | bytes 589856 | tf_op jit(solution)/shard_map/ppermute | solution.py:17
  86.3 11.7 %cholesky.216 = f32[128,128]{1,0:T(8,128)S(1)} custom-call(f32[128,128]{1,0:T(8,128)S(1)} %fusion.107), custom_call_target="Cholesky" | custom-call | tf_op jit(solution)/shard_map/jit(cholesky)/cholesky | solution.py:34
  99.4 9.8 %custom-call.57 = f32[1,128,128]{1,2,0:T(8,128)S(1)} custom-call(f32[1,128,128]{2,1,0:T(8,128)S(1)} %fusion.63), custom_call_target="InvertDiagBlocksLowerTriangular" | custom-call | tf_op jit(solution)/shard_map/triangular_solve/custom-call.2 | solution.py:22
  110.4 11.7 %cholesky.227 = f32[128,128]{1,0:T(8,128)S(1)} custom-call(f32[128,128]{1,0:T(8,128)S(1)} %fusion.104), custom_call_target="Cholesky" | custom-call | tf_op jit(solution)/shard_map/jit(cholesky)/cholesky | solution.py:36
  123.5 21.7 %custom-call.39 = f32[1,128,128]{1,2,0:T(8,128)S(1)} custom-call(f32[1,128,128]{2,1,0:T(8,128)S(1)} %fusion.64), custom_call_target="InvertDiagBlocksLowerTriangular" | custom-call | tf_op jit(solution)/shard_map/triangular_solve | solution.py:22
  147.5 2.4 add_convert_fusion
  151.3 4.1 collective-permute-start.1
  155.4 7.0 collective-permute-done.1
  162.5 12.1 %collective-permute-start.2 = (f32[128,1024]{0,1:T(8,128)S(1)}, f32[128,1024]{0,1:T(8,128)}, u32[]{:S(2)}, u32[]{:S(2)}) collective-permute-start(f32[128,1024]{0,1:T(8,128)S(1)} %add.125), channel_id=1, source_target_pairs={{0,64},{32,96},{64,0},{96,32},{128,192},{160,224},{192,128},{224,1... | collective-permute-start | bytes 1572872 | tf_op jit(solution)/shard_map/ppermute | solution.py:17
  174.6 22.9 %collective-permute-done.2 = f32[128,1024]{0,1:T(8,128)} collective-permute-done((f32[128,1024]{0,1:T(8,128)S(1)}, f32[128,1024]{0,1:T(8,128)}, u32[]{:S(2)}, u32[]{:S(2)}) %collective-permute-start.2) | collective-permute-done | bytes 524320 | tf_op jit(solution)/shard_map/ppermute | solution.py:17
  198.8 11.7 %cholesky.238 = f32[128,128]{1,0:T(8,128)S(1)} custom-call(f32[128,128]{1,0:T(8,128)S(1)} %fusion.100), custom_call_target="Cholesky" | custom-call | tf_op jit(solution)/shard_map/jit(cholesky)/cholesky | solution.py:34
  211.8 9.8 %custom-call.59 = f32[1,128,128]{1,2,0:T(8,128)S(1)} custom-call(f32[1,128,128]{2,1,0:T(8,128)S(1)} %fusion.65), custom_call_target="InvertDiagBlocksLowerTriangular" | custom-call | tf_op jit(solution)/shard_map/triangular_solve/custom-call.2 | solution.py:22
  222.9 11.7 %cholesky.249 = f32[128,128]{1,0:T(8,128)S(1)} custom-call(f32[128,128]{1,0:T(8,128)S(1)} %fusion.97), custom_call_target="Cholesky" | custom-call | tf_op jit(solution)/shard_map/jit(cholesky)/cholesky | solution.py:36
  235.9 10.2 %custom-call.40 = f32[1,128,128]{1,2,0:T(8,128)S(1)} custom-call(f32[1,128,128]{2,1,0:T(8,128)S(1)} %fusion.66), custom_call_target="InvertDiagBlocksLowerTriangular" | custom-call | tf_op jit(solution)/shard_map/triangular_solve | solution.py:22
  248.2 2.2 add_convert_fusion.1
  251.1 2.8 collective-permute-start.3
  253.9 9.9 %collective-permute-done.3 = f32[128,896]{0,1:T(8,128)S(1)} collective-permute-done((f32[128,896]{0,1:T(8,128)S(1)}, f32[128,896]{0,1:T(8,128)S(1)}, u32[]{:S(2)}, u32[]{:S(2)}) %collective-permute-start.3) | collective-permute-done | bytes 458784 | tf_op jit(solution)/shard_map/ppermute | solution.py:17
  263.9 5.5 collective-permute-start.4
  269.4 19.9 %collective-permute-done.4 = f32[128,896]{0,1:T(8,128)S(1)} collective-permute-done((f32[128,896]{0,1:T(8,128)S(1)}, f32[128,896]{0,1:T(8,128)S(1)}, u32[]{:S(2)}, u32[]{:S(2)}) %collective-permute-start.4) | collective-permute-done | bytes 458784 | tf_op jit(solution)/shard_map/ppermute | solution.py:17
  289.4 8.8 %collective-permute-start.5 = (f32[128,896]{0,1:T(8,128)S(1)}, f32[128,896]{0,1:T(8,128)S(1)}, u32[]{:S(2)}, u32[]{:S(2)}) collective-permute-start(f32[128,896]{0,1:T(8,128)S(1)} %add.130), channel_id=1, source_target_pairs={{0,128},{32,160},{64,192},{96,224},{128,0},{160,32},{192,64},{224,... | collective-permute-start | bytes 1376264 | tf_op jit(solution)/shard_map/ppermute | solution.py:17
  298.2 39.4 %collective-permute-done.5 = f32[128,896]{0,1:T(8,128)S(1)} collective-permute-done((f32[128,896]{0,1:T(8,128)S(1)}, f32[128,896]{0,1:T(8,128)S(1)}, u32[]{:S(2)}, u32[]{:S(2)}) %collective-permute-start.5) | collective-permute-done | bytes 458784 | tf_op jit(solution)/shard_map/ppermute | solution.py:17
  337.8 11.7 %cholesky.260 = f32[128,128]{1,0:T(8,128)S(1)} custom-call(f32[128,128]{1,0:T(8,128)S(1)} %fusion.93), custom_call_target="Cholesky" | custom-call | tf_op jit(solution)/shard_map/jit(cholesky)/cholesky | solution.py:34
  350.9 9.8 %custom-call.61 = f32[1,128,128]{1,2,0:T(8,128)S(1)} custom-call(f32[1,128,128]{2,1,0:T(8,128)S(1)} %fusion.67), custom_call_target="InvertDiagBlocksLowerTriangular" | custom-call | tf_op jit(solution)/shard_map/triangular_solve/custom-call.2 | solution.py:22
  361.9 11.7 %cholesky.271 = f32[128,128]{1,0:T(8,128)S(1)} custom-call(f32[128,128]{1,0:T(8,128)S(1)} %fusion.90), custom_call_target="Cholesky" | custom-call | tf_op jit(solution)/shard_map/jit(cholesky)/cholesky | solution.py:36
  374.9 9.9 %custom-call.41 = f32[1,128,128]{1,2,0:T(8,128)S(1)} custom-call(f32[1,128,128]{2,1,0:T(8,128)S(1)} %fusion.68), custom_call_target="InvertDiagBlocksLowerTriangular" | custom-call | tf_op jit(solution)/shard_map/triangular_solve | solution.py:22
  386.7 2.1 add_convert_fusion.2
  389.4 1.9 collective-permute-start.6
  391.3 10.2 %collective-permute-done.6 = f32[128,768]{0,1:T(8,128)S(1)} collective-permute-done((f32[128,768]{0,1:T(8,128)S(1)}, f32[128,768]{0,1:T(8,128)S(1)}, u32[]{:S(2)}, u32[]{:S(2)}) %collective-permute-start.6) | collective-permute-done | bytes 393248 | tf_op jit(solution)/shard_map/ppermute | solution.py:17
  401.5 1.9 collective-permute-start.7
  403.5 20.3 %collective-permute-done.7 = f32[128,768]{0,1:T(8,128)S(1)} collective-permute-done((f32[128,768]{0,1:T(8,128)S(1)}, f32[128,768]{0,1:T(8,128)S(1)}, u32[]{:S(2)}, u32[]{:S(2)}) %collective-permute-start.7) | collective-permute-done | bytes 393248 | tf_op jit(solution)/shard_map/ppermute | solution.py:17
  423.8 4.3 collective-permute-start.8
  428.2 35.9 %collective-permute-done.8 = f32[128,768]{0,1:T(8,128)S(1)} collective-permute-done((f32[128,768]{0,1:T(8,128)S(1)}, f32[128,768]{0,1:T(8,128)S(1)}, u32[]{:S(2)}, u32[]{:S(2)}) %collective-permute-start.8) | collective-permute-done | bytes 393248 | tf_op jit(solution)/shard_map/ppermute | solution.py:17
  464.9 19.1 %collective-permute-start.9 = (f32[128,768]{0,1:T(8,128)}, f32[128,768]{0,1:T(8,128)}, u32[]{:S(2)}, u32[]{:S(2)}) collective-permute-start(f32[128,768]{0,1:T(8,128)} %add.136), channel_id=1, source_target_pairs={{0,256},{32,288},{64,320},{96,352},{128,384},{160,416},{192,448},{... | collective-permute-start | bytes 1179656 | tf_op jit(solution)/shard_map/ppermute | solution.py:17
  484.0 14.5 %collective-permute-done.9 = f32[128,768]{0,1:T(8,128)} collective-permute-done((f32[128,768]{0,1:T(8,128)}, f32[128,768]{0,1:T(8,128)}, u32[]{:S(2)}, u32[]{:S(2)}) %collective-permute-start.9) | collective-permute-done | bytes 393248 | tf_op jit(solution)/shard_map/ppermute | solution.py:17
  498.5 1.9 broadcast_select_fusion.7
  501.1 1.6 copy.24
  504.1 13.2 %cholesky.282 = f32[128,128]{1,0:T(8,128)} custom-call(f32[128,128]{1,0:T(8,128)} %fusion.86), custom_call_target="Cholesky" | custom-call | tf_op jit(solution)/shard_map/jit(cholesky)/cholesky | solution.py:34
  518.8 2.1 fusion.69
  520.9 11.3 %custom-call.63 = f32[1,128,128]{1,2,0:T(8,128)} custom-call(f32[1,128,128]{2,1,0:T(8,128)} %fusion.69), custom_call_target="InvertDiagBlocksLowerTriangular" | custom-call | tf_op jit(solution)/shard_map/triangular_solve/custom-call.2 | solution.py:22
  533.3 2.1 convolution_subtract_fusion.9
  535.4 1.8 convolution_subtract_fusion.13
  537.2 1.6 copy.26
  540.3 13.2 %cholesky.293 = f32[128,128]{1,0:T(8,128)} custom-call(f32[128,128]{1,0:T(8,128)} %fusion.83), custom_call_target="Cholesky" | custom-call | tf_op jit(solution)/shard_map/jit(cholesky)/cholesky | solution.py:36
  555.0 2.1 fusion.70
  557.1 11.6 %custom-call.42 = f32[1,128,128]{1,2,0:T(8,128)} custom-call(f32[1,128,128]{2,1,0:T(8,128)} %fusion.70), custom_call_target="InvertDiagBlocksLowerTriangular" | custom-call | tf_op jit(solution)/shard_map/triangular_solve | solution.py:22
  576.2 98.2 %all-gather.3.cloned.1.call-done = f32[2048,640]{0,1:T(8,128)} async-done(((f32[128,640]{0,1:T(8,128)}), f32[2048,640]{0,1:T(8,128)}) %all-gather.3.cloned.1.call-update) | async-done | bytes 5242896 | tf_op jit(solution)/shard_map/all_gather | solution.py:11
  674.4 3.7 copy.45
  678.9 15.3 %collective-permute-start.10 = (f32[128,640]{0,1:T(8,128)S(1)}, f32[128,640]{0,1:T(8,128)S(1)}, u32[]{:S(2)}, u32[]{:S(2)}) collective-permute-start(f32[128,640]{0,1:T(8,128)S(1)} %bitcast_reduce_fusion), channel_id=1, source_target_pairs={{0,1},{1,0},{2,3},{3,2},{4,5},{5,4},{6,7},{7,6},{8,9},{9,8},{10,11... | collective-permute-start | bytes 983048 | tf_op jit(solution)/shard_map/ppermute | solution.py:17
  695.6 11.7 %cholesky.304 = f32[128,128]{1,0:T(8,128)S(1)} custom-call(f32[128,128]{1,0:T(8,128)S(1)} %fusion.79), custom_call_target="Cholesky" | custom-call | tf_op jit(solution)/shard_map/jit(cholesky)/cholesky | solution.py:34
  708.7 9.8 %custom-call.65 = f32[1,128,128]{1,2,0:T(8,128)S(1)} custom-call(f32[1,128,128]{2,1,0:T(8,128)S(1)} %fusion.71), custom_call_target="InvertDiagBlocksLowerTriangular" | custom-call | tf_op jit(solution)/shard_map/triangular_solve/custom-call.2 | solution.py:22
  719.6 11.7 %cholesky.315 = f32[128,128]{1,0:T(8,128)S(1)} custom-call(f32[128,128]{1,0:T(8,128)S(1)} %fusion.76), custom_call_target="Cholesky" | custom-call | tf_op jit(solution)/shard_map/jit(cholesky)/cholesky | solution.py:36
  732.6 10.0 %custom-call.43 = f32[1,128,128]{1,2,0:T(8,128)S(1)} custom-call(f32[1,128,128]{2,1,0:T(8,128)S(1)} %fusion.72), custom_call_target="InvertDiagBlocksLowerTriangular" | custom-call | tf_op jit(solution)/shard_map/triangular_solve | solution.py:22
  744.0 2.7 add_convert_fusion.4
  (132 shorter events, 56.6 us)
Async XLA Ops:
  6.5 667.8 %all-gather.3.cloned.1.call-start = ((), (), s32[]{:S(2)}) async-start(), calls=%async_computation | async-start | bytes 5570560 | tf_op jit(solution)/shard_map/all_gather | solution.py:11
  14.8 0.8 copy-start.5
  71.1 2.0 copy-start
  73.1 12.9 %collective-permute-start = (f32[128,1152]{0,1:T(8,128)S(1)}, f32[128,1152]{0,1:T(8,128)S(1)}, u32[]{:S(2)}, u32[]{:S(2)}) collective-permute-start(f32[128,1152]{0,1:T(8,128)S(1)} %convolution_bitcast_fusion), channel_id=1, source_target_pairs={{0,32},{32,0},{64,96},{96,64},{128,160},{160,128},{192,224},{224,1... | collective-permute-start | bytes 1769480 | tf_op jit(solution)/shard_map/ppermute | solution.py:17
  146.9 3.0 copy-start.1
  149.9 1.4 copy-start.2
  151.3 11.1 %collective-permute-start.1 = (f32[128,1024]{0,1:T(8,128)S(1)}, f32[128,1024]{0,1:T(8,128)S(1)}, u32[]{:S(2)}, u32[]{:S(2)}) collective-permute-start(f32[128,1024]{0,1:T(8,128)S(1)} %convolution_bitcast_fusion.1), channel_id=1, source_target_pairs={{0,32},{32,0},{64,96},{96,64},{128,160},{160,128},{192,224},{224,1... | collective-permute-start | bytes 1572872 | tf_op jit(solution)/shard_map/ppermute | solution.py:17
  162.5 35.0 %collective-permute-start.2 = (f32[128,1024]{0,1:T(8,128)S(1)}, f32[128,1024]{0,1:T(8,128)}, u32[]{:S(2)}, u32[]{:S(2)}) collective-permute-start(f32[128,1024]{0,1:T(8,128)S(1)} %add.125), channel_id=1, source_target_pairs={{0,64},{32,96},{64,0},{96,32},{128,192},{160,224},{192,128},{224,1... | collective-permute-start | bytes 1572872 | tf_op jit(solution)/shard_map/ppermute | solution.py:17
  250.4 39.0 %copy-start.3 = (bf16[1024,896]{1,0:T(8,128)(2,1)}, bf16[1024,896]{1,0:T(8,128)(2,1)S(1)}, u32[]{:S(2)}) copy-start(bf16[1024,896]{1,0:T(8,128)(2,1)S(1)} %add_convert_fusion.1) | copy-start | bytes 5505028
  251.1 12.7 %collective-permute-start.3 = (f32[128,896]{0,1:T(8,128)S(1)}, f32[128,896]{0,1:T(8,128)S(1)}, u32[]{:S(2)}, u32[]{:S(2)}) collective-permute-start(f32[128,896]{0,1:T(8,128)S(1)} %convolution_bitcast_fusion.2), channel_id=1, source_target_pairs={{0,32},{32,0},{64,96},{96,64},{128,160},{160,128},{192,224},{224,1... | collective-permute-start | bytes 1376264 | tf_op jit(solution)/shard_map/ppermute | solution.py:17
  263.9 25.4 %collective-permute-start.4 = (f32[128,896]{0,1:T(8,128)S(1)}, f32[128,896]{0,1:T(8,128)S(1)}, u32[]{:S(2)}, u32[]{:S(2)}) collective-permute-start(f32[128,896]{0,1:T(8,128)S(1)} %add.129), channel_id=1, source_target_pairs={{0,64},{32,96},{64,0},{96,32},{128,192},{160,224},{192,128},{224,1... | collective-permute-start | bytes 1376264 | tf_op jit(solution)/shard_map/ppermute | solution.py:17
  289.4 48.3 %collective-permute-start.5 = (f32[128,896]{0,1:T(8,128)S(1)}, f32[128,896]{0,1:T(8,128)S(1)}, u32[]{:S(2)}, u32[]{:S(2)}) collective-permute-start(f32[128,896]{0,1:T(8,128)S(1)} %add.130), channel_id=1, source_target_pairs={{0,128},{32,160},{64,192},{96,224},{128,0},{160,32},{192,64},{224,... | collective-permute-start | bytes 1376264 | tf_op jit(solution)/shard_map/ppermute | solution.py:17
  389.4 12.1 %collective-permute-start.6 = (f32[128,768]{0,1:T(8,128)S(1)}, f32[128,768]{0,1:T(8,128)S(1)}, u32[]{:S(2)}, u32[]{:S(2)}) collective-permute-start(f32[128,768]{0,1:T(8,128)S(1)} %convolution_bitcast_fusion.3), channel_id=1, source_target_pairs={{0,32},{32,0},{64,96},{96,64},{128,160},{160,128},{192,224},{224,1... | collective-permute-start | bytes 1179656 | tf_op jit(solution)/shard_map/ppermute | solution.py:17
  401.5 22.2 %collective-permute-start.7 = (f32[128,768]{0,1:T(8,128)S(1)}, f32[128,768]{0,1:T(8,128)S(1)}, u32[]{:S(2)}, u32[]{:S(2)}) collective-permute-start(f32[128,768]{0,1:T(8,128)S(1)} %add.134), channel_id=1, source_target_pairs={{0,64},{32,96},{64,0},{96,32},{128,192},{160,224},{192,128},{224,1... | collective-permute-start | bytes 1179656 | tf_op jit(solution)/shard_map/ppermute | solution.py:17
  423.8 40.2 %collective-permute-start.8 = (f32[128,768]{0,1:T(8,128)S(1)}, f32[128,768]{0,1:T(8,128)S(1)}, u32[]{:S(2)}, u32[]{:S(2)}) collective-permute-start(f32[128,768]{0,1:T(8,128)S(1)} %add.135), channel_id=1, source_target_pairs={{0,128},{32,160},{64,192},{96,224},{128,0},{160,32},{192,64},{224,... | collective-permute-start | bytes 1179656 | tf_op jit(solution)/shard_map/ppermute | solution.py:17
  464.9 33.7 %collective-permute-start.9 = (f32[128,768]{0,1:T(8,128)}, f32[128,768]{0,1:T(8,128)}, u32[]{:S(2)}, u32[]{:S(2)}) collective-permute-start(f32[128,768]{0,1:T(8,128)} %add.136), channel_id=1, source_target_pairs={{0,256},{32,288},{64,320},{96,352},{128,384},{160,416},{192,448},{... | collective-permute-start | bytes 1179656 | tf_op jit(solution)/shard_map/ppermute | solution.py:17
  573.8 1.1 copy-start.4
  678.9 16.5 %collective-permute-start.10 = (f32[128,640]{0,1:T(8,128)S(1)}, f32[128,640]{0,1:T(8,128)S(1)}, u32[]{:S(2)}, u32[]{:S(2)}) collective-permute-start(f32[128,640]{0,1:T(8,128)S(1)} %bitcast_reduce_fusion), channel_id=1, source_target_pairs={{0,1},{1,0},{2,3},{3,2},{4,5},{5,4},{6,7},{7,6},{8,9},{9,8},{10,11... | collective-permute-start | bytes 983048 | tf_op jit(solution)/shard_map/ppermute | solution.py:17
Sparse Core Ops, SparseCore 0:
  576.3 98.0 all-gather.2
